TPU v7x, 32 devices: a whole 2x2x4 slice. The times are simulated.
32 devices in a mesh: dp: 16 (over z, y, core), tensor: 2 (over x).
Axes of the slice: x: 2, y: 2, z: 4, core: 2. Of those that a mesh axis runs over, the one named last changes fastest.
Arguments:
- block_input: bfloat16 [160, 197, 768], P('dp'), may hold values from -6 to 6
- image_counts: int32 [16], P('dp'), may hold values from 1 to 10, 88 in all
- first_norm_gain: float32 [768], replicated, may hold values from 0.1 to 1.9
- first_norm_bias: float32 [768], replicated, may hold values from -3 to 3
- w_qkv: bfloat16 [3, 768, 768], P(None, None, 'tensor'), may hold values from -8 to 8
- qv_bias: float32 [2, 768], P(None, 'tensor'), may hold values from -3 to 3
- w_out: bfloat16 [768, 768], P('tensor'), may hold values from -0.75 to 0.75
- b_out: float32 [768], replicated, may hold values from -3 to 3
- second_norm_gain: float32 [768], replicated, may hold values from 0.1 to 1.9
- second_norm_bias: float32 [768], replicated, may hold values from -3 to 3
- w_fc1: bfloat16 [768, 3072], P(None, 'tensor'), may hold values from -0.21875 to 0.21875
- b_fc1: float32 [3072], P('tensor'), may hold values from -3 to 3
- w_fc2: bfloat16 [3072, 768], P('tensor'), may hold values from -0.109375 to 0.109375
- b_fc2: float32 [768], replicated, may hold values from -3 to 3
- cotangent: bfloat16 [160, 197, 768], P('dp'), may hold values from -6 to 6
Outputs:
- block_out: bfloat16 [160, 197, 768], P('dp')
- gradient_of_input: bfloat16 [160, 197, 768], P('dp')
- first_norm_gain_gradient: float32 [768], replicated
- grad_ln1_bias: float32 [768], replicated
- grad_w_qkv: float32 [3, 768, 768], P(None, None, 'tensor')
- grad_qv_bias: float32 [2, 768], P(None, 'tensor')
- grad_w_out: float32 [768, 768], P('tensor')
- grad_b_out: float32 [768], replicated
- second_norm_gain_gradient: float32 [768], replicated
- grad_ln2_bias: float32 [768], replicated
- grad_w_fc1: float32 [768, 3072], P(None, 'tensor')
- grad_b_fc1: float32 [3072], P('tensor')
- grad_w_fc2: float32 [3072, 768], P('tensor')
- grad_b_fc2: float32 [768], replicated
All inputs are finite; a program needn't handle non-finite values. No bound on the sum of `image_counts` on one device may be relied on, other than what follows from the above.
Results may differ from a plain program's by a relative error of at most 0.012.
The roundings to bfloat16 on the way count: a program that leaves them out, or rounds other values in their place, can miss the bound.
Values sent between devices are 32-bit elements; how exact they have to be, the bound alone decides.
No kernel may reach another device: no remote copies, remote signals or barrier semaphores. Data moves between devices by JAX's collectives and lax.ppermute only.
A program may use at most 256 MiB of HBM per device.

v0:
```python
import jax
import jax.numpy as jnp
from jax import lax
from jax.sharding import PartitionSpec as P

HD = 64
EPSILON = 1e-06
INV_ROOT2 = 0.7071067811865476
INV_ROOT2PI = 0.3989422804014327


def apply_layer_norm(values, norm_gain, norm_bias):
    center = jnp.mean(values, -1, keepdims=True)
    shifted = values - center
    spread = jnp.mean(shifted * shifted, -1, keepdims=True)
    inv_std = lax.rsqrt(spread + EPSILON)
    normed = shifted * inv_std
    return (normed * norm_gain + norm_bias, normed, inv_std)


def norm_backward_pass(grad_normed, normed, inv_std, norm_gain):
    scaled = grad_normed * norm_gain
    first = jnp.mean(scaled, -1, keepdims=True)
    second = jnp.mean(scaled * normed, -1, keepdims=True)
    return inv_std * (scaled - first - normed * second)


def gelu_value(pre_act):
    return 0.5 * pre_act * (1.0 + lax.erf(pre_act * INV_ROOT2))


def gelu_slope(pre_act):
    return (
        0.5 * (1.0 + lax.erf(pre_act * INV_ROOT2))
        + pre_act * jnp.exp(-0.5 * pre_act * pre_act) * INV_ROOT2PI
    )


def head_scores(queries, keys_all, scale):
    return (
        jnp.einsum("ishd,ithd->ihst", queries, keys_all, preferred_element_type=jnp.float32) * scale
    )


def shards(
    block_input,
    image_counts,
    first_norm_gain,
    first_norm_bias,
    w_qkv,
    qv_bias,
    w_out,
    b_out,
    second_norm_gain,
    second_norm_bias,
    w_fc1,
    b_fc1,
    w_fc2,
    b_fc2,
    cotangent,
):
    float_thirtytwo = jnp.float32
    bfloat_sixteen = jnp.bfloat16
    image_batch, sequence_length, model_width = block_input.shape
    total_rows = image_batch * sequence_length
    local_heads = w_qkv.shape[2] // HD
    local_width = local_heads * HD
    scale = HD ** (-0.5)
    shape4 = (image_batch, sequence_length, local_heads, HD)
    live_rows = (jnp.arange(total_rows, dtype=jnp.int32) // sequence_length < image_counts[0])[
        :, None
    ]
    input_tokens = block_input.reshape(total_rows, model_width).astype(float_thirtytwo)
    first_normed_tokens, first_centered_scaled, first_inverse_deviation = apply_layer_norm(
        input_tokens, first_norm_gain, first_norm_bias
    )
    normed_one_b = first_normed_tokens.astype(bfloat_sixteen)
    projected = jnp.einsum(
        "nd,cde->cne", normed_one_b, w_qkv, preferred_element_type=float_thirtytwo
    )
    queries = (projected[0] + qv_bias[0]).astype(bfloat_sixteen).reshape(shape4)
    keys_all = projected[1].astype(bfloat_sixteen).reshape(shape4)
    values_all = (projected[2] + qv_bias[1]).astype(bfloat_sixteen).reshape(shape4)
    scores = head_scores(queries, keys_all, scale)
    log_total = jax.nn.logsumexp(scores, axis=-1)
    probs = jnp.exp(scores - log_total[..., None]).astype(bfloat_sixteen)
    context = (
        jnp.einsum("ihst,ithd->ishd", probs, values_all, preferred_element_type=float_thirtytwo)
        .astype(bfloat_sixteen)
        .reshape(total_rows, local_width)
    )
    attn_part = jnp.dot(context, w_out, preferred_element_type=float_thirtytwo)
    attn_full = lax.psum(attn_part, "tensor")
    residual_stream = input_tokens + (attn_full + b_out)
    second_normed_tokens, second_centered_scaled, second_inverse_deviation = apply_layer_norm(
        residual_stream, second_norm_gain, second_norm_bias
    )
    normed_two_b = second_normed_tokens.astype(bfloat_sixteen)
    pre_act = jnp.dot(normed_two_b, w_fc1, preferred_element_type=float_thirtytwo) + b_fc1
    activated = gelu_value(pre_act).astype(bfloat_sixteen)
    mlp_part = jnp.dot(activated, w_fc2, preferred_element_type=float_thirtytwo)
    mlp_full = lax.psum(mlp_part, "tensor")
    outputs = residual_stream + (mlp_full + b_fc2)
    block_out = (
        jnp.where(live_rows, outputs, 0.0)
        .astype(bfloat_sixteen)
        .reshape(image_batch, sequence_length, model_width)
    )
    output_gradient = jnp.where(
        live_rows, cotangent.reshape(total_rows, model_width), jnp.zeros((), bfloat_sixteen)
    )
    grad_w_fc2 = jnp.einsum(
        "nf,nd->fd", activated, output_gradient, preferred_element_type=float_thirtytwo
    )
    grad_b_fc2 = jnp.sum(output_gradient.astype(float_thirtytwo), axis=0)
    grad_act = jnp.einsum(
        "nd,fd->nf", output_gradient, w_fc2, preferred_element_type=float_thirtytwo
    )
    grad_pre = (grad_act * gelu_slope(pre_act)).astype(bfloat_sixteen)
    grad_w_fc1 = jnp.einsum(
        "nd,nf->df", normed_two_b, grad_pre, preferred_element_type=float_thirtytwo
    )
    grad_b_fc1 = jnp.sum(grad_pre.astype(float_thirtytwo), axis=0)
    norm_two_part = jnp.einsum("nf,df->nd", grad_pre, w_fc1, preferred_element_type=float_thirtytwo)
    second_normed_gradient = lax.psum(norm_two_part, "tensor")
    second_norm_gain_gradient = jnp.sum(second_normed_gradient * second_centered_scaled, axis=0)
    grad_ln2_bias = jnp.sum(second_normed_gradient, axis=0)
    residual_gradient = output_gradient.astype(float_thirtytwo) + norm_backward_pass(
        second_normed_gradient, second_centered_scaled, second_inverse_deviation, second_norm_gain
    )
    grad_resid_b = residual_gradient.astype(bfloat_sixteen)
    grad_w_out = jnp.einsum(
        "ne,nd->ed", context, grad_resid_b, preferred_element_type=float_thirtytwo
    )
    grad_b_out = jnp.sum(residual_gradient, axis=0)
    grad_context = (
        jnp.einsum("nd,ed->ne", grad_resid_b, w_out, preferred_element_type=float_thirtytwo)
        .astype(bfloat_sixteen)
        .reshape(shape4)
    )
    probs_full = jnp.exp(head_scores(queries, keys_all, scale) - log_total[..., None])
    probs_again = probs_full.astype(bfloat_sixteen)
    grad_values = jnp.einsum(
        "ihst,ishd->ithd", probs_again, grad_context, preferred_element_type=float_thirtytwo
    ).astype(bfloat_sixteen)
    grad_probs = jnp.einsum(
        "ishd,ithd->ihst", grad_context, values_all, preferred_element_type=float_thirtytwo
    )
    row_dot = jnp.sum(probs_full * grad_probs, axis=-1, keepdims=True)
    grad_scores = (probs_full * (grad_probs - row_dot)).astype(bfloat_sixteen)
    grad_queries = (
        jnp.einsum("ihst,ithd->ishd", grad_scores, keys_all, preferred_element_type=float_thirtytwo)
        * scale
    ).astype(bfloat_sixteen)
    grad_keys = (
        jnp.einsum("ihst,ishd->ithd", grad_scores, queries, preferred_element_type=float_thirtytwo)
        * scale
    ).astype(bfloat_sixteen)
    grad_proj = jnp.stack([grad_queries, grad_keys, grad_values]).reshape(
        3, total_rows, local_width
    )
    grad_w_qkv = jnp.einsum(
        "nd,cne->cde", normed_one_b, grad_proj, preferred_element_type=float_thirtytwo
    )
    grad_qv_bias = jnp.stack(
        [
            jnp.sum(grad_proj[0].astype(float_thirtytwo), axis=0),
            jnp.sum(grad_proj[2].astype(float_thirtytwo), axis=0),
        ]
    )
    norm_one_part = jnp.einsum(
        "cne,cde->nd", grad_proj, w_qkv, preferred_element_type=float_thirtytwo
    )
    first_normed_gradient = lax.psum(norm_one_part, "tensor")
    first_norm_gain_gradient = jnp.sum(first_normed_gradient * first_centered_scaled, axis=0)
    grad_ln1_bias = jnp.sum(first_normed_gradient, axis=0)
    gradient_of_input = (
        (
            residual_gradient
            + norm_backward_pass(
                first_normed_gradient,
                first_centered_scaled,
                first_inverse_deviation,
                first_norm_gain,
            )
        )
        .astype(bfloat_sixteen)
        .reshape(image_batch, sequence_length, model_width)
    )
    summed = lax.psum(
        (
            first_norm_gain_gradient,
            grad_ln1_bias,
            grad_w_qkv,
            grad_qv_bias,
            grad_w_out,
            grad_b_out,
            second_norm_gain_gradient,
            grad_ln2_bias,
            grad_w_fc1,
            grad_b_fc1,
            grad_w_fc2,
            grad_b_fc2,
        ),
        "dp",
    )
    first_norm_gain_gradient, grad_ln1_bias, grad_w_qkv, grad_qv_bias, grad_w_out, grad_b_out = (
        summed[0],
        summed[1],
        summed[2],
        summed[3],
        summed[4],
        summed[5],
    )
    second_norm_gain_gradient, grad_ln2_bias, grad_w_fc1, grad_b_fc1, grad_w_fc2, grad_b_fc2 = (
        summed[6],
        summed[7],
        summed[8],
        summed[9],
        summed[10],
        summed[11],
    )
    return (
        block_out,
        gradient_of_input,
        first_norm_gain_gradient,
        grad_ln1_bias,
        grad_w_qkv,
        grad_qv_bias,
        grad_w_out,
        grad_b_out,
        second_norm_gain_gradient,
        grad_ln2_bias,
        grad_w_fc1,
        grad_b_fc1,
        grad_w_fc2,
        grad_b_fc2,
    )


def solution(mesh):
    in_specs = (
        P("dp", None, None),
        P("dp"),
        P(),
        P(),
        P(None, None, "tensor"),
        P(None, "tensor"),
        P("tensor", None),
        P(),
        P(),
        P(),
        P(None, "tensor"),
        P("tensor"),
        P("tensor", None),
        P(),
        P("dp", None, None),
    )
    out_specs = (
        P("dp", None, None),
        P("dp", None, None),
        P(),
        P(),
        P(None, None, "tensor"),
        P(None, "tensor"),
        P("tensor", None),
        P(),
        P(),
        P(),
        P(None, "tensor"),
        P("tensor"),
        P("tensor", None),
        P(),
    )
    return jax.shard_map(shards, mesh=mesh, in_specs=in_specs, out_specs=out_specs, check_vma=False)
```

profile of v0, /device:TPU:0, one launch (start us, length us, event | category | flops | bytes accessed | tf_op | source)
XLA Modules:
  0.0 1190.0 jit_solution(15098997224716500326)
XLA Ops:
  7.3 6.9 reshape.188
  19.7 7.4 convolution_bitcast_fusion
  35.0 8.1 squeeze.14
  68.9 8.1 squeeze.13
  80.2 8.9 convert_bitcast_fusion.1
  108.5 146.6 %all-reduce.8.cloned.1.call-done = f32[1970,768]{1,0:T(8,128)} async-done(((f32[1970,768]{1,0:T(8,128)}), f32[1970,768]{1,0:T(8,128)}) %all-reduce.8.cloned.1.call-update) | async-done | bytes 6051856 | tf_op jit(solution)/shard_map/psum | solution.py:93
  261.3 8.0 multiply_convert_fusion.1
  269.4 9.3 convert_reduce_fusion
  281.2 6.8 fusion.39
  288.1 10.1 fusion.29
  298.2 8.9 fusion.32
  307.1 130.0 %all-reduce.10.cloned.1.call-done = f32[1970,768]{1,0:T(8,128)} async-done(((f32[1970,768]{1,0:T(8,128)}), f32[1970,768]{1,0:T(8,128)}) %all-reduce.10.cloned.1.call-update) | async-done | bytes 6051856 | tf_op jit(solution)/shard_map/psum | solution.py:125
  464.0 8.5 convert_reduce_fusion.2
  472.5 12.1 %multiply_reduce_fusion = (f32[10,6,197]{2,1,0:T(8,128)S(1)}, f32[10,6,197,197]{2,3,1,0:T(8,128)}) fusion(f32[10,6,197,197]{2,3,1,0:T(8,128)} %copy-done.2, f32[10,6,197]{2,1,0:T(8,128)S(1)} %log_add_fusion, bf16[10,197,6,64]{1,3,2,0:T(8,128)(2,1)S(1)} %copy.49, bf16[10,197,6,64]{1,0,3,2:T(8,128)(2,1)} %copy-done.11), kind=kOutput, calls=%fused_computation.2 | convolution fusion | flops 307355456 | bytes 21748800 | tf_op jit(solution)/shard_map/ishd,ithd->ihst/dot_general | solution.py:146
  484.6 6.5 multiply_convert_fusion
  526.9 6.1 reshape.191
  538.6 9.1 convolution_bitcast_fusion.2
  547.8 11.2 fusion.38
  559.0 6.2 convolution_bitcast_fusion.1
  567.7 236.9 %all-reduce.12.cloned.1.call-done = (f32[3,768,384]{1,2,0:T(8,128)}, f32[384,768]{1,0:T(8,128)}, f32[768,1536]{1,0:T(8,128)}, f32[1536,768]{1,0:T(8,128)}) async-done(((f32[3,768,384]{1,2,0:T(8,128)}, f32[384,768]{1,0:T(8,128)}, f32[768,1536]{1,0:T(8,128)}, f32[1536,768]{1,0:T(8,128)}), (f32[3,768,384]{1,2,0:T(8,128)}, f32[384,768]{1,0:T(8,128)}, f32[768,1536]{1,0:T(8,128)}, ...) | async-done | bytes 14155792 | tf_op jit(solution)/shard_map/psum | solution.py:190
  809.7 275.8 %all-reduce.14.cloned.1.call-done = (f32[1970,768]{1,0:T(8,128)}, f32[1970,768]{1,0:T(8,128)}) async-done(((f32[1970,768]{1,0:T(8,128)}, f32[1970,768]{1,0:T(8,128)}), (f32[1970,768]{1,0:T(8,128)}, f32[1970,768]{1,0:T(8,128)})) %all-reduce.14.cloned.1.call-update) | async-done | bytes 12103696 | tf_op jit(solution)/shard_map/psum | solution.py:102
  1091.8 6.7 add_convert_fusion.2
  1102.6 6.6 select_convert_fusion
  1113.3 61.7 %all-reduce = (f32[768]{0:T(1024)}, f32[768]{0:T(1024)}, f32[2,384]{1,0:T(2,128)}, f32[768]{0:T(1024)}, f32[768]{0:T(1024)}, /*index=5*/f32[768]{0:T(1024)}, f32[1536]{0:T(1024)}, f32[768]{0:T(1024)}) all-reduce(f32[768]{0:T(1024)S(1)} %get-tuple-element.44, ...), channel_id=1, replica_groups=mesh['dp'=16,'tensor'=2] {'dp'}, use_global_device_ids=true, to_apply=%region_16.17 | all-reduce | flops 6912 | bytes 55296 | tf_op jit(solution)/shard_map/psum | solution.py:190
  (157 shorter events, 168.3 us)
Async XLA Ops:
  7.2 254.1 %copy-start = (bf16[768,1536]{1,0:T(8,128)(2,1)S(1)}, bf16[768,1536]{1,0:T(8,128)(2,1)}, u32[]{:S(2)}) copy-start(bf16[768,1536]{1,0:T(8,128)(2,1)} %param.25) | copy-start | bytes 7077892
  7.2 12.5 %copy-start.24 = (f32[768]{0:T(1024)S(1)}, f32[768]{0:T(1024)}, u32[]{:S(2)}) copy-start(f32[768]{0:T(1024)} %param.17) | copy-start | bytes 9220
  7.2 12.5 %copy-start.34 = (f32[768]{0:T(1024)S(1)}, f32[768]{0:T(1024)}, u32[]{:S(2)}) copy-start(f32[768]{0:T(1024)} %param.18) | copy-start | bytes 9220
  7.2 247.9 %all-reduce.8.cloned.1.call-start = ((), (), s32[]{:S(2)}) async-start(), calls=%async_computation | async-start | bytes 12140544 | tf_op jit(solution)/shard_map/psum | solution.py:93
  89.0 9.0 copy-start.16
  103.7 151.4 %copy-start.27 = (f32[768]{0:T(1024)S(1)}, f32[768]{0:T(1024)}, u32[]{:S(2)}) copy-start(f32[768]{0:T(1024)} %param.22) | copy-start | bytes 9220
  103.8 333.4 %all-reduce.10.cloned.1.call-start = ((), (), s32[]{:S(2)}) async-start(), calls=%async_computation.1 | async-start | bytes 12140544 | tf_op jit(solution)/shard_map/psum | solution.py:125
  260.4 9.0 copy-start.3
  288.0 516.6 %all-reduce.12.cloned.1.call-start = ((), (), s32[]{:S(2)}) async-start(), calls=%async_computation.2 | async-start | bytes 28311552 | tf_op jit(solution)/shard_map/psum | solution.py:190
  288.1 10.2 copy-start.37
  463.9 20.6 %slice-start = ((s8[12288000]{0:T(1024)(128)(4,1)}), s8[4194304]{0:T(1024)(128)(4,1)S(1)}, s32[]{:S(2)}) async-start(s8[12288000]{0:T(1024)(128)(4,1)} %bitcast.49), calls=%async_computation.4 | async-start | bytes 8388608
  464.0 20.6 %slice-start.1 = ((s8[12288000]{0:T(1024)(128)(4,1)}), s8[4194304]{0:T(1024)(128)(4,1)S(1)}, s32[]{:S(2)}) async-start(s8[12288000]{0:T(1024)(128)(4,1)} %bitcast.49), calls=%async_computation.5 | async-start | bytes 8388608
  472.5 12.1 %slice-start.2 = ((s8[12288000]{0:T(1024)(128)(4,1)}), s8[3899392]{0:T(1024)(128)(4,1)S(1)}, s32[]{:S(2)}) async-start(s8[12288000]{0:T(1024)(128)(4,1)} %bitcast.49), calls=%async_computation.6 | async-start | bytes 7798784
  510.6 11.9 %copy-start.12 = (bf16[10,197,6,64]{1,3,2,0:T(8,128)(2,1)S(1)}, bf16[10,197,6,64]{1,3,2,0:T(8,128)(2,1)}, u32[]{:S(2)}) copy-start(bf16[10,197,6,64]{1,3,2,0:T(8,128)(2,1)} %get-tuple-element.81) | copy-start | bytes 4538884
  526.8 9.3 copy-start.15
  526.8 11.8 copy-start.21
  526.8 11.8 copy-start.23
  526.8 11.8 copy-start.25
  526.8 11.8 copy-start.35
  547.8 537.8 %all-reduce.14.cloned.1.call-start = ((), (), s32[]{:S(2)}) async-start(), calls=%async_computation.3 | async-start | bytes 24281088 | tf_op jit(solution)/shard_map/psum | solution.py:102
  547.8 11.2 copy-start.19
  547.8 11.2 copy-start.31
  1109.1 65.9 %copy-start.17 = (f32[384,768]{1,0:T(8,128)S(1)}, f32[384,768]{1,0:T(8,128)}, u32[]{:S(2)}) copy-start(f32[384,768]{1,0:T(8,128)} %get-tuple-element.92) | copy-start | bytes 3538948
  1113.3 67.8 %slice-start.3 = ((s8[4718592]{0:T(1024)(128)(4,1)}), s8[524288]{0:T(1024)(128)(4,1)S(1)}, s32[]{:S(2)}) async-start(s8[4718592]{0:T(1024)(128)(4,1)} %bitcast.51), calls=%async_computation.7 | async-start | bytes 1048576
  (23 other events, 116.2 us)
Sparse Core Ops, SparseCore 0:
  103.9 151.1 all-reduce.7
  288.2 148.9 all-reduce.9
  547.9 256.6 all-reduce.11
  806.9 278.5 all-reduce.13
where the time goes:
time: 1200 us; the launch traced here: 1190 us
  waiting for transfers between devices  789 us (66%)
  local copies, waits for them, and re-layouts  135 us (11%)
  matrix products  127 us (11%)
  blocking collectives  61.7 us (5%)
  other arithmetic  61 us (5%)
  between operations  15.2 us (1%)
    psum x1, waiting for transfers between devices, shards(): mlp_full = lax.psum(mlp_part, 'tensor')  276 us
    psum x1, waiting for transfers between devices, shards(): lax.psum((first_norm_gain_gradient, grad_ln1_bias, grad_w_qkv, grad_qv_bi...  237 us
    psum x1, waiting for transfers between devices, shards(): attn_full = lax.psum(attn_part, 'tensor')  147 us
    psum x1, waiting for transfers between devices, shards(): second_normed_gradient = lax.psum(norm_two_part, 'tensor')  130 us
    psum x1, blocking collectives, shards(): lax.psum((first_norm_gain_gradient, grad_ln1_bias, grad_w_qkv, grad_qv_bi...  61.7 us
    another operation x7, local copies, waits for them, and re-layouts, shards(): jnp.stack([grad_queries, grad_keys, grad_values])  34.4 us
    unnamed x92, local copies, waits for them, and re-layouts  24.3 us
  transfers between devices with their start and end apart: 4, of which 4 were waited for; matrix products, arithmetic and copies ran while one was open for 4% of the time, Pallas kernels for 0%

commit v1 on v0

--- a/solution.py
+++ b/solution.py
@@ -99,7 +99,7 @@
     pre_act = jnp.dot(normed_two_b, w_fc1, preferred_element_type=float_thirtytwo) + b_fc1
     activated = gelu_value(pre_act).astype(bfloat_sixteen)
     mlp_part = jnp.dot(activated, w_fc2, preferred_element_type=float_thirtytwo)
-    mlp_full = lax.psum(mlp_part, "tensor")
+    mlp_full = jnp.sum(lax.all_gather(mlp_part, "tensor"), axis=0)
     outputs = residual_stream + (mlp_full + b_fc2)
     block_out = (
         jnp.where(live_rows, outputs, 0.0)

time: 1200 us -> 1130 us (0.942)
  waiting for transfers between devices: 789 us -> 719 us
    psum x1, waiting for transfers between devices: 276 us -> 111 us  [shards(): first_normed_gradient = lax.psum(norm_one_part, 'tensor')]
    all_gather x0 -> x1, waiting for transfers between devices: none -> 144 us  [shards(): mlp_full = jnp.sum(lax.all_gather(mlp_part, 'tensor'), axis=0)]
    psum x1, waiting for transfers between devices: 237 us -> 181 us  [shards(): lax.psum((first_norm_gain_gradient, grad_ln1_bias, grad_w_qkv, grad_qv_bi...]
    unnamed x92 -> x98, local copies, waits for them, and re-layouts: 24.3 us -> 26.4 us
  transfers between devices with their start and end apart: 4 -> 5, of which waited for: 4 -> 5; matrix products, arithmetic and copies ran while one was open for 4% -> 7% of each run, Pallas kernels for 0% -> 0%
where the time goes in v1:
time: 1130 us
  waiting for transfers between devices  719 us (64%)
  local copies, waits for them, and re-layouts  137 us (12%)
  matrix products  120 us (11%)
  other arithmetic  69.2 us (6%)
  blocking collectives  65.1 us (6%)
  between operations  15.5 us (1%)
    psum x1, waiting for transfers between devices, shards(): lax.psum((first_norm_gain_gradient, grad_ln1_bias, grad_w_qkv, grad_qv_bi...  181 us
    psum x1, waiting for transfers between devices, shards(): attn_full = lax.psum(attn_part, 'tensor')  146 us
    all_gather x1, waiting for transfers between devices, shards(): mlp_full = jnp.sum(lax.all_gather(mlp_part, 'tensor'), axis=0)  144 us
    psum x1, waiting for transfers between devices, shards(): second_normed_gradient = lax.psum(norm_two_part, 'tensor')  138 us
    psum x1, waiting for transfers between devices, shards(): first_normed_gradient = lax.psum(norm_one_part, 'tensor')  111 us
    psum x1, blocking collectives, shards(): lax.psum((first_norm_gain_gradient, grad_ln1_bias, grad_w_qkv, grad_qv_bi...  65.1 us
    another operation x7, local copies, waits for them, and re-layouts, shards(): jnp.stack([grad_queries, grad_keys, grad_values])  34.1 us
    unnamed x98, local copies, waits for them, and re-layouts  26.4 us
  transfers between devices with their start and end apart: 5, of which 5 were waited for; matrix products, arithmetic and copies ran while one was open for 7% of the time, Pallas kernels for 0%

profile of v1, /device:TPU:0, one launch (start us, length us, event | category | flops | bytes accessed | tf_op | source)
XLA Modules:
  0.0 1126.0 jit_solution(15803106053272681122)
XLA Ops:
  12.8 6.7 reshape.188
  19.7 7.4 convolution_bitcast_fusion
  46.5 8.1 squeeze.14
  58.2 8.1 squeeze.13
  102.5 146.4 %all-reduce.7.cloned.1.call-done = f32[1970,768]{1,0:T(8,128)} async-done(((f32[1970,768]{1,0:T(8,128)}), f32[1970,768]{1,0:T(8,128)}) %all-reduce.7.cloned.1.call-update) | async-done | bytes 6051856 | tf_op jit(solution)/shard_map/psum | solution.py:93
  255.1 8.0 multiply_convert_fusion.1
  263.1 9.3 convert_reduce_fusion
  275.0 6.7 fusion.38
  283.4 9.4 convolution_bitcast_fusion.2
  292.9 138.0 %all-reduce.9.cloned.1.call-done = f32[1970,768]{1,0:T(8,128)} async-done(((f32[1970,768]{1,0:T(8,128)}), f32[1970,768]{1,0:T(8,128)}) %all-reduce.9.cloned.1.call-update) | async-done | bytes 6051856 | tf_op jit(solution)/shard_map/psum | solution.py:125
  430.9 6.2 multiply_reduce_fusion.3
  437.1 143.5 %all-gather.4.cloned.1.call-done = f32[2,1970,768]{2,1,0:T(8,128)} async-done(((f32[1,1970,768]{2,1,0:T(8,128)}), f32[2,1970,768]{2,1,0:T(8,128)}) %all-gather.4.cloned.1.call-update) | async-done | bytes 12103696 | tf_op jit(solution)/shard_map/all_gather | solution.py:102
  580.7 8.5 reduce_sum.185
  589.2 10.4 fusion.34
  612.5 8.6 convert_reduce_fusion.2
  621.1 12.2 %multiply_reduce_fusion = (f32[10,6,197]{2,1,0:T(8,128)S(1)}, f32[10,6,197,197]{2,3,1,0:T(8,128)}) fusion(f32[10,6,197,197]{2,3,1,0:T(8,128)} %copy-done.2, f32[10,6,197]{2,1,0:T(8,128)S(1)} %log_add_fusion, bf16[10,197,6,64]{1,3,2,0:T(8,128)(2,1)S(1)} %copy.73, bf16[10,197,6,64]{1,0,3,2:T(8,128)(2,1)} %copy-done.10), kind=kOutput, calls=%fused_computation.2 | convolution fusion | flops 307355456 | bytes 21748800 | tf_op jit(solution)/shard_map/ishd,ithd->ihst/dot_general | solution.py:146
  633.4 6.5 multiply_convert_fusion
  693.6 9.9 fusion.29
  703.5 12.3 %fusion.32 = f32[768,1536]{1,0:T(8,128)} fusion(bf16[1970,1536]{1,0:T(8,128)(2,1)} %copy-done.34, f32[1970,768]{1,0:T(8,128)} %copy-done.4, f32[768]{0:T(1024)S(1)} %copy-done.31, f32[768]{0:T(1024)S(1)} %copy-done.21, f32[1970]{0:T(1024)S(1)} %add_rsqrt_fusion.1, f32[1970]{0:T(1024)S(1)} %broadcast_multiply_fusion.5), kind=kOutput, calls=%fused_computation.94 | convolution fusion | flops 4655377920 | bytes 16844176 | tf_op jit(solution)/shard_map/nd,nf->df/dot_general | solution.py:120
  718.4 6.4 convolution_bitcast_fusion.3
  731.5 110.6 %all-reduce.11.cloned.1.call-done = f32[1970,768]{1,0:T(8,128)} async-done(((f32[1970,768]{1,0:T(8,128)}), f32[1970,768]{1,0:T(8,128)}) %all-reduce.11.cloned.1.call-update) | async-done | bytes 6051856 | tf_op jit(solution)/shard_map/psum | solution.py:174
  848.4 6.8 add_convert_fusion.2
  859.2 65.1 %all-reduce = (f32[768]{0:T(1024)}, f32[768]{0:T(1024)}, f32[2,384]{1,0:T(2,128)}, f32[768]{0:T(1024)}, f32[768]{0:T(1024)}, /*index=5*/f32[768]{0:T(1024)}, f32[1536]{0:T(1024)}, f32[768]{0:T(1024)}) all-reduce(f32[768]{0:T(1024)S(1)} %get-tuple-element.58, ...), channel_id=1, replica_groups=mesh['dp'=16,'tensor'=2] {'dp'}, use_global_device_ids=true, to_apply=%region_16.17 | all-reduce | flops 6912 | bytes 55296 | tf_op jit(solution)/shard_map/psum | solution.py:190
  924.3 180.8 %all-reduce.13.cloned.1.call-done = (f32[3,768,384]{1,2,0:T(8,128)}, f32[384,768]{1,0:T(8,128)}, f32[768,1536]{1,0:T(8,128)}, f32[1536,768]{1,0:T(8,128)}) async-done(((f32[3,768,384]{1,2,0:T(8,128)}, f32[384,768]{1,0:T(8,128)}, f32[768,1536]{1,0:T(8,128)}, f32[1536,768]{1,0:T(8,128)}), (f32[3,768,384]{1,2,0:T(8,128)}, f32[384,768]{1,0:T(8,128)}, f32[768,1536]{1,0:T(8,128)}, ...) | async-done | bytes 14155792 | tf_op jit(solution)/shard_map/psum | solution.py:190
  (169 shorter events, 174.3 us)
Async XLA Ops:
  7.2 247.8 %copy-start = (bf16[768,1536]{1,0:T(8,128)(2,1)S(1)}, bf16[768,1536]{1,0:T(8,128)(2,1)}, u32[]{:S(2)}) copy-start(bf16[768,1536]{1,0:T(8,128)(2,1)} %param.25) | copy-start | bytes 7077892
  7.2 241.6 %all-reduce.7.cloned.1.call-start = ((), (), s32[]{:S(2)}) async-start(), calls=%async_computation | async-start | bytes 12140544 | tf_op jit(solution)/shard_map/psum | solution.py:93
  9.9 9.8 copy-start.17
  9.9 9.8 copy-start.22
  9.9 9.8 copy-start.32
  97.5 151.4 %copy-start.24 = (f32[768]{0:T(1024)S(1)}, f32[768]{0:T(1024)}, u32[]{:S(2)}) copy-start(f32[768]{0:T(1024)} %param.22) | copy-start | bytes 9220
  97.5 333.4 %all-reduce.9.cloned.1.call-start = ((), (), s32[]{:S(2)}) async-start(), calls=%async_computation.1 | async-start | bytes 12140544 | tf_op jit(solution)/shard_map/psum | solution.py:125
  254.1 9.0 copy-start.4
  281.8 298.9 %all-gather.4.cloned.1.call-start = ((), (), s32[]{:S(2)}) async-start(), calls=%async_computation.3 | async-start | bytes 18210816 | tf_op jit(solution)/shard_map/all_gather | solution.py:102
  292.8 549.3 %all-reduce.11.cloned.1.call-start = ((), (), s32[]{:S(2)}) async-start(), calls=%async_computation.2 | async-start | bytes 12140544 | tf_op jit(solution)/shard_map/psum | solution.py:174
  437.1 152.0 %copy-start.25 = (f32[768]{0:T(1024)S(1)}, f32[768]{0:T(1024)}, u32[]{:S(2)}) copy-start(f32[768]{0:T(1024)} %param.28) | copy-start | bytes 9220
  612.5 20.8 %slice-start = ((s8[12288000]{0:T(1024)(128)(4,1)}), s8[4194304]{0:T(1024)(128)(4,1)S(1)}, s32[]{:S(2)}) async-start(s8[12288000]{0:T(1024)(128)(4,1)} %bitcast.51), calls=%async_computation.5 | async-start | bytes 8388608
  612.5 20.8 %slice-start.1 = ((s8[12288000]{0:T(1024)(128)(4,1)}), s8[4194304]{0:T(1024)(128)(4,1)S(1)}, s32[]{:S(2)}) async-start(s8[12288000]{0:T(1024)(128)(4,1)} %bitcast.51), calls=%async_computation.6 | async-start | bytes 8388608
  621.1 12.3 %slice-start.2 = ((s8[12288000]{0:T(1024)(128)(4,1)}), s8[3899392]{0:T(1024)(128)(4,1)S(1)}, s32[]{:S(2)}) async-start(s8[12288000]{0:T(1024)(128)(4,1)} %bitcast.51), calls=%async_computation.7 | async-start | bytes 7798784
  659.4 11.9 %copy-start.11 = (bf16[10,197,6,64]{1,3,2,0:T(8,128)(2,1)S(1)}, bf16[10,197,6,64]{1,3,2,0:T(8,128)(2,1)}, u32[]{:S(2)}) copy-start(bf16[10,197,6,64]{1,3,2,0:T(8,128)(2,1)} %get-tuple-element.94) | copy-start | bytes 4538884
  675.4 9.5 copy-start.13
  693.5 411.6 %all-reduce.13.cloned.1.call-start = ((), (), s32[]{:S(2)}) async-start(), calls=%async_computation.4 | async-start | bytes 28311552 | tf_op jit(solution)/shard_map/psum | solution.py:190
  693.6 22.3 %slice-start.3 = ((s8[6070272]{0:T(1024)(128)(4,1)}), s8[4194304]{0:T(1024)(128)(4,1)S(1)}, s32[]{:S(2)}) async-start(s8[6070272]{0:T(1024)(128)(4,1)} %bitcast.53), calls=%async_computation.8 | async-start | bytes 8388608
  693.6 24.8 %slice-start.5 = ((s8[6070272]{0:T(1024)(128)(4,1)}), s8[4194304]{0:T(1024)(128)(4,1)S(1)}, s32[]{:S(2)}) async-start(s8[6070272]{0:T(1024)(128)(4,1)} %bitcast.55), calls=%async_computation.10 | async-start | bytes 8388608
  693.6 24.8 %slice-start.9 = ((s8[4552704]{0:T(1024)(128)(4,1)}), s8[4194304]{0:T(1024)(128)(4,1)S(1)}, s32[]{:S(2)}) async-start(s8[4552704]{0:T(1024)(128)(4,1)} %bitcast.59), calls=%async_computation.14 | async-start | bytes 8388608
  703.5 12.4 %slice-start.4 = ((s8[6070272]{0:T(1024)(128)(4,1)}), s8[1875968]{0:T(1024)(128)(4,1)S(1)}, s32[]{:S(2)}) async-start(s8[6070272]{0:T(1024)(128)(4,1)} %bitcast.53), calls=%async_computation.9 | async-start | bytes 3751936
  703.5 12.4 %copy-start.8 = (bf16[1970,384]{0,1:T(8,128)(2,1)S(1)}, bf16[1970,384]{0,1:T(8,128)(2,1)}, u32[]{:S(2)}) copy-start(bf16[1970,384]{0,1:T(8,128)(2,1)} %reshape.183) | copy-start | bytes 4538884
  703.5 14.8 %slice-start.6 = ((s8[6070272]{0:T(1024)(128)(4,1)}), s8[1875968]{0:T(1024)(128)(4,1)S(1)}, s32[]{:S(2)}) async-start(s8[6070272]{0:T(1024)(128)(4,1)} %bitcast.55), calls=%async_computation.11 | async-start | bytes 3751936
  703.5 14.8 %slice-start.10 = ((s8[4552704]{0:T(1024)(128)(4,1)}), s8[358400]{0:T(1024)(128)(4,1)S(1)}, s32[]{:S(2)}) async-start(s8[4552704]{0:T(1024)(128)(4,1)} %bitcast.59), calls=%async_computation.15 | async-start | bytes 716800
  (27 other events, 115.8 us)
Sparse Core Ops, SparseCore 0:
  97.6 151.1 all-reduce.6
  281.9 148.9 all-reduce.8
  432.5 148.1 all-gather.3
  693.6 148.4 all-reduce.10
  847.7 257.3 all-reduce.12
